TPU v7x, 32 devices: a whole 2x2x4 slice. The times are simulated.
32 devices in a mesh: gz: 8 (over z, y), xy: 4 (over x, core).
Axes of the slice: x: 2, y: 2, z: 4, core: 2. Of those that a mesh axis runs over, the one named last changes fastest.
Arguments:
- up_source: bfloat16 [8, 2, 32, 1024], P('gz', None, None, 'xy'), may hold values from -6 to 6
- down_source: bfloat16 [8, 2, 32, 1024], P('gz', None, None, 'xy'), may hold values from -6 to 6
- source_layer: int32 [32], replicated, may hold values from 0 to 7, as said below
- u_factor: bfloat16 [8, 4, 4, 2, 128, 256], P('gz', 'xy'), may hold values from -0.15625 to 0.15625
- v_factor: bfloat16 [8, 4, 4, 2, 128, 256], P('gz', 'xy'), may hold values from -0.25 to 0.25
- block_rank: int32 [8, 4, 4], P('gz', 'xy'), may hold values from 1 to 4
Outputs:
- up_trace: bfloat16 [8, 2, 32, 1024], P('gz', None, None, 'xy')
- down_trace: bfloat16 [8, 2, 32, 1024], P('gz', None, None, 'xy')
Inputs may be any that keep to these rules, and one draw needn't show every extreme that they name: `source_layer`: the index of the layer slab in which source s lies; source 0 lies in slab 0 and source 1 in slab 8 - 1. `block_rank`: block (i, j) of interface l has rank 32 times this number.
All inputs are finite; a program needn't handle non-finite values.
Results may differ from a plain program's by a relative error of at most 0.007.
Values may be sent and summed in bfloat16 or wider, within the bound.
A program may use at most 64 MiB of HBM per device.

v0:
```python
import jax
import jax.numpy as jnp
from jax import lax
from jax.sharding import PartitionSpec as P

STEPS = 3


def from_behind(block, axis, distance):
    devices = range(lax.axis_size(axis))
    route = [(i - distance, i) for i in devices if i - distance in devices]
    return lax.ppermute(block, axis, route)


def complex_parts(product):
    real = product[..., 0, :, 0, :] - product[..., 1, :, 1, :]
    imag = product[..., 0, :, 1, :] + product[..., 1, :, 0, :]
    return jnp.stack([real, imag], axis=-3)


def advance(up_part, down_part, active_up, active_down, u_layer, v_layer, keep_rank, v_columns):
    sources = up_part.shape[1]
    own_rows = u_layer.shape[0]
    blocks = u_layer.shape[1]
    width = u_layer.shape[-1]
    gathered = lax.all_gather(up_part, "xy", axis=2, tiled=True)
    pieces = gathered.reshape(2, sources, blocks, width)
    up_coef = complex_parts(
        jnp.einsum("asjb,ijcrb->ijascr", pieces, v_layer, preferred_element_type=jnp.float32)
    )
    up_coef = jnp.where(keep_rank[:, :, None, None, :], up_coef, 0.0).astype(jnp.bfloat16)
    forward = complex_parts(
        jnp.einsum("ijasr,ijcrb->iascb", up_coef, u_layer, preferred_element_type=jnp.float32)
    )
    forward = jnp.transpose(forward, (1, 2, 0, 3)).reshape(2, sources, own_rows * width)
    arrived = from_behind(forward, "gz", 1)
    new_up = (active_up.astype(jnp.float32) + arrived).astype(jnp.bfloat16)
    upper = from_behind(down_part, "gz", -1)
    upper_blocks = upper.reshape(2, sources, own_rows, width)
    down_coef = complex_parts(
        jnp.einsum("asib,ijcrb->ijascr", upper_blocks, u_layer, preferred_element_type=jnp.float32)
    )
    down_coef = jnp.where(keep_rank[:, :, None, None, :], down_coef, 0.0).astype(jnp.bfloat16)
    column_coef = lax.all_to_all(down_coef, "xy", split_axis=1, concat_axis=0, tiled=True)
    summed = complex_parts(
        jnp.einsum("ijasr,ijcrb->jascb", column_coef, v_columns, preferred_element_type=jnp.float32)
    )
    backward = jnp.transpose(summed, (1, 2, 0, 3)).reshape(2, sources, own_rows * width)
    new_down = (active_down.astype(jnp.float32) + backward).astype(jnp.bfloat16)
    return (new_up, new_down)


def on_device(up_source, down_source, source_layer, u_factor, v_factor, block_rank):
    layer_index = lax.axis_index("gz")
    up_mask = (layer_index >= source_layer)[None, :, None]
    down_mask = (layer_index <= source_layer)[None, :, None]
    active_up = jnp.where(up_mask, up_source[0], jnp.zeros_like(up_source[0]))
    active_down = jnp.where(down_mask, down_source[0], jnp.zeros_like(down_source[0]))
    u_layer = u_factor[0]
    v_layer = v_factor[0]
    rank_units = block_rank[0]
    max_rank = u_layer.shape[-2]
    keep_rank = (
        jnp.arange(max_rank, dtype=jnp.int32)[None, None, :]
        < max_rank // 4 * rank_units[:, :, None]
    )
    v_columns = lax.all_to_all(v_layer, "xy", split_axis=1, concat_axis=0, tiled=True)
    up_trace = active_up
    down_trace = active_down
    for sweep_index in range(STEPS):
        up_trace, down_trace = advance(
            up_trace, down_trace, active_up, active_down, u_layer, v_layer, keep_rank, v_columns
        )
    return (up_trace[None], down_trace[None])


def solution(mesh):
    in_specs = (
        P("gz", None, None, "xy"),
        P("gz", None, None, "xy"),
        P(),
        P("gz", "xy", None, None, None, None),
        P("gz", "xy", None, None, None, None),
        P("gz", "xy", None),
    )
    out_specs = (P("gz", None, None, "xy"), P("gz", None, None, "xy"))
    return jax.shard_map(
        on_device, mesh=mesh, in_specs=in_specs, out_specs=out_specs, check_vma=False
    )
```

profile of v0, /device:TPU:0, one launch (start us, length us, event | category | flops | bytes accessed | tf_op | source)
XLA Modules:
  0.0 86.9 jit_solution(7317015157043258093)
XLA Ops:
  0.6 0.0 copy-start
  0.6 0.0 copy-start.3
  0.7 0.7 copy-done.3
  1.4 0.0 copy-start.1
  1.4 0.8 bitcast_select_fusion
  2.2 1.3 %collective-permute-start.3 = (bf16[2,32,256]{2,1,0:T(8,128)(2,1)S(1)}, bf16[2,32,256]{2,1,0:T(8,128)(2,1)S(1)}, u32[]{:S(2)}, u32[]{:S(2)}) collective-permute-start(bf16[2,32,256]{2,1,0:T(8,128)(2,1)S(1)} %bitcast_select_fusion), channel_id=1, source_target_pairs={{4,0},{8,4},{12,8},{16,12},{20,16},{24,20},{28,24},{5,1},{9,5},{13... | collective-permute-start | bytes 98312 | tf_op jit(solution)/shard_map/ppermute | solution.py:12
  3.5 0.0 copy-done.1
  3.5 0.1 bitcast_select_fusion.1
  3.6 6.5 %all_gather.9 = bf16[2,32,1024]{2,1,0:T(8,128)(2,1)S(1)} all-gather(bf16[2,32,256]{2,1,0:T(8,128)(2,1)S(1)} %bitcast_select_fusion.1), channel_id=1, replica_groups=mesh['gz'=8,'xy'=4] {'xy'}, dimensions={2}, use_global_device_ids=true | all-gather | bytes 163840 | tf_op jit(solution)/shard_map/all_gather | solution.py:26
  10.1 0.1 reshape.884
  10.2 1.3 %convolution_bitcast_fusion.5 = f32[1,4,2,32,2,128]{5,3,4,2,1,0:T(8,128)S(1)} fusion(bf16[1,1,4,2,128,256]{5,4,3,2,1,0:T(8,128)(2,1)} %param.10, bf16[2,32,4,256,1]{3,2,1,0,4:T(4,128)(2,1)S(1)} %bitcast.274), kind=kOutput, calls=%fused_computation.5 | convolution fusion | flops 33554432 | bytes 917504 | tf_op jit(solution)/shard_map/asjb,ijcrb->ijascr/dot_general | solution.py:29
  11.5 0.0 copy-start.4
  11.5 0.6 copy-done.4
  12.2 0.1 iota_compare_fusion
  12.2 0.0 copy-done
  12.2 0.2 convolution_bitcast_fusion.11
  12.5 4.5 %collective-permute-start = (f32[2,32,256]{2,1,0:T(8,128)S(1)}, f32[2,32,256]{2,1,0:T(8,128)S(1)}, u32[]{:S(2)}, u32[]{:S(2)}) collective-permute-start(f32[2,32,256]{2,1,0:T(8,128)S(1)} %maximum_bitcast_fusion), channel_id=1, source_target_pairs={{0,4},{4,8},{8,12},{12,16},{16,20},{20,24},{24,28},{1,5},{5,9},{9,... | collective-permute-start | bytes 196616 | tf_op jit(solution)/shard_map/ppermute | solution.py:12
  17.0 0.0 collective-permute-done.3
  17.1 0.3 convolution_bitcast_fusion.2
  17.4 1.6 %collective-permute-done = f32[2,32,256]{2,1,0:T(8,128)S(1)} collective-permute-done((f32[2,32,256]{2,1,0:T(8,128)S(1)}, f32[2,32,256]{2,1,0:T(8,128)S(1)}, u32[]{:S(2)}, u32[]{:S(2)}) %collective-permute-start) | collective-permute-done | bytes 65568 | tf_op jit(solution)/shard_map/ppermute | solution.py:12
  18.9 0.1 fusion.33
  19.0 5.4 %all_gather.10 = bf16[2,32,1024]{2,1,0:T(8,128)(2,1)S(1)} all-gather(bf16[2,32,256]{2,1,0:T(8,128)(2,1)S(1)} %fusion.33), channel_id=1, replica_groups=mesh['gz'=8,'xy'=4] {'xy'}, dimensions={2}, use_global_device_ids=true | all-gather | bytes 163840 | tf_op jit(solution)/shard_map/all_gather | solution.py:26
  24.4 0.1 reshape.887
  24.5 1.3 %convolution_bitcast_fusion.4 = f32[1,4,2,32,2,128]{5,3,1,4,2,0:T(8,128)S(1)} fusion(bf16[2,32,4,256,1]{3,2,1,0,4:T(4,128)(2,1)S(1)} %bitcast.275, bf16[1,1,4,2,128,256]{5,4,3,2,1,0:T(8,128)(2,1)} %param.10), kind=kOutput, calls=%fused_computation.4 | convolution fusion | flops 33554432 | bytes 917504 | tf_op jit(solution)/shard_map/asjb,ijcrb->ijascr/dot_general | solution.py:29
  25.8 0.2 convolution_bitcast_fusion.10
  26.1 4.7 %collective-permute-start.1 = (f32[2,32,256]{2,1,0:T(8,128)S(1)}, f32[2,32,256]{2,1,0:T(8,128)S(1)}, u32[]{:S(2)}, u32[]{:S(2)}) collective-permute-start(f32[2,32,256]{2,1,0:T(8,128)S(1)} %maximum_bitcast_fusion.1), channel_id=1, source_target_pairs={{0,4},{4,8},{8,12},{12,16},{16,20},{20,24},{24,28},{1,5},{5,9},{9,... | collective-permute-start | bytes 196616 | tf_op jit(solution)/shard_map/ppermute | solution.py:12
  30.8 0.6 copy.49
  31.4 3.3 %all-to-all-start = ((bf16[1,4,2,32,128]{4,3,2,0,1:T(8,128)(2,1)}), bf16[1,4,2,32,128]{4,3,2,0,1:T(8,128)(2,1)S(1)}, u32[]{:S(2)}, u32[]{:S(2)}) async-start(bf16[1,4,2,32,128]{4,3,2,0,1:T(8,128)(2,1)} %copy.49), calls=%async_computation | async-start | bytes 131072 | tf_op jit(solution)/shard_map/all_to_all | solution.py:44
  34.7 0.0 collective-permute-done.1
  34.7 0.1 fusion.34
  34.8 4.0 %all-to-all-done = bf16[1,4,2,32,128]{4,3,2,0,1:T(8,128)(2,1)S(1)} async-done(((bf16[1,4,2,32,128]{4,3,2,0,1:T(8,128)(2,1)}), bf16[1,4,2,32,128]{4,3,2,0,1:T(8,128)(2,1)S(1)}, u32[]{:S(2)}, u32[]{:S(2)}) %all-to-all-start) | async-done | bytes 65568 | tf_op jit(solution)/shard_map/all_to_all | solution.py:44
  38.8 3.5 %all-to-all-start.1 = ((bf16[1,4,2,128,256]{4,3,2,0,1:T(8,128)(2,1)}), bf16[1,4,2,128,256]{4,3,2,0,1:T(8,128)(2,1)S(1)}, u32[]{:S(2)}, u32[]{:S(2)}) async-start(bf16[1,4,2,128,256]{4,3,2,0,1:T(8,128)(2,1)} %bitcast.74), calls=%async_computation.1 | async-start | bytes 1048576 | tf_op jit(solution)/shard_map/all_to_all | solution.py:67
  42.3 10.3 %all_gather.11 = bf16[2,32,1024]{2,1,0:T(8,128)(2,1)S(1)} all-gather(bf16[2,32,256]{2,1,0:T(8,128)(2,1)S(1)} %fusion.34), channel_id=1, replica_groups=mesh['gz'=8,'xy'=4] {'xy'}, dimensions={2}, use_global_device_ids=true | all-gather | bytes 163840 | tf_op jit(solution)/shard_map/all_gather | solution.py:26
  52.6 0.1 reshape.888
  52.7 1.3 %convolution_bitcast_fusion.3 = f32[1,4,2,32,2,128]{5,3,1,4,2,0:T(8,128)S(1)} fusion(bf16[2,32,4,256,1]{3,2,1,0,4:T(4,128)(2,1)S(1)} %bitcast.276, bf16[1,1,4,2,128,256]{5,4,3,2,1,0:T(8,128)(2,1)} %param.10), kind=kOutput, calls=%fused_computation.3 | convolution fusion | flops 33554432 | bytes 917504 | tf_op jit(solution)/shard_map/asjb,ijcrb->ijascr/dot_general | solution.py:29
  54.0 0.0 all-to-all-done.1
  54.1 0.2 convolution_bitcast_fusion.8
  54.3 0.0 copy-start.2
  54.3 0.7 copy-done.2
  55.0 0.1 fusion.31
  55.1 1.3 %collective-permute-start.4 = (bf16[2,32,256]{2,1,0:T(8,128)(2,1)S(1)}, bf16[2,32,256]{2,1,0:T(8,128)(2,1)S(1)}, u32[]{:S(2)}, u32[]{:S(2)}) collective-permute-start(bf16[2,32,256]{2,1,0:T(8,128)(2,1)S(1)} %fusion.31), channel_id=1, source_target_pairs={{4,0},{8,4},{12,8},{16,12},{20,16},{24,20},{28,24},{5,1},{9,5},{13... | collective-permute-start | bytes 98312 | tf_op jit(solution)/shard_map/ppermute | solution.py:12
  56.4 0.2 convolution_bitcast_fusion.9
  56.6 5.6 %collective-permute-done.4 = bf16[2,32,256]{2,1,0:T(8,128)(2,1)S(1)} collective-permute-done((bf16[2,32,256]{2,1,0:T(8,128)(2,1)S(1)}, bf16[2,32,256]{2,1,0:T(8,128)(2,1)S(1)}, u32[]{:S(2)}, u32[]{:S(2)}) %collective-permute-start.4) | collective-permute-done | bytes 32800 | tf_op jit(solution)/shard_map/ppermute | solution.py:12
  62.2 0.3 convolution_bitcast_fusion.1
  62.6 0.6 copy.53
  63.2 3.3 %all-to-all-start.2 = ((bf16[1,4,2,32,128]{4,3,2,0,1:T(8,128)(2,1)}), bf16[1,4,2,32,128]{4,3,2,0,1:T(8,128)(2,1)S(1)}, u32[]{:S(2)}, u32[]{:S(2)}) async-start(bf16[1,4,2,32,128]{4,3,2,0,1:T(8,128)(2,1)} %copy.53), calls=%async_computation.2 | async-start | bytes 131072 | tf_op jit(solution)/shard_map/all_to_all | solution.py:44
  66.5 4.1 %all-to-all-done.2 = bf16[1,4,2,32,128]{4,3,2,0,1:T(8,128)(2,1)S(1)} async-done(((bf16[1,4,2,32,128]{4,3,2,0,1:T(8,128)(2,1)}), bf16[1,4,2,32,128]{4,3,2,0,1:T(8,128)(2,1)S(1)}, u32[]{:S(2)}, u32[]{:S(2)}) %all-to-all-start.2) | async-done | bytes 65568 | tf_op jit(solution)/shard_map/all_to_all | solution.py:44
  70.6 0.2 convolution_bitcast_fusion.7
  70.8 0.1 fusion.32
  70.9 1.3 %collective-permute-start.5 = (bf16[2,32,256]{2,1,0:T(8,128)(2,1)S(1)}, bf16[2,32,256]{2,1,0:T(8,128)(2,1)S(1)}, u32[]{:S(2)}, u32[]{:S(2)}) collective-permute-start(bf16[2,32,256]{2,1,0:T(8,128)(2,1)S(1)} %fusion.32), channel_id=1, source_target_pairs={{4,0},{8,4},{12,8},{16,12},{20,16},{24,20},{28,24},{5,1},{9,5},{13... | collective-permute-start | bytes 98312 | tf_op jit(solution)/shard_map/ppermute | solution.py:12
  72.2 5.5 %collective-permute-start.2 = (f32[2,32,256]{2,1,0:T(8,128)S(1)}, f32[2,32,256]{2,1,0:T(8,128)S(1)}, u32[]{:S(2)}, u32[]{:S(2)}) collective-permute-start(f32[2,32,256]{2,1,0:T(8,128)S(1)} %maximum_bitcast_fusion.2), channel_id=1, source_target_pairs={{0,4},{4,8},{8,12},{12,16},{16,20},{20,24},{24,28},{1,5},{5,9},{9,... | collective-permute-start | bytes 196616 | tf_op jit(solution)/shard_map/ppermute | solution.py:12
  77.6 0.0 collective-permute-done.5
  77.6 0.3 convolution_bitcast_fusion
  78.0 0.6 copy.56
  78.6 3.3 %all-to-all-start.3 = ((bf16[1,4,2,32,128]{4,3,2,0,1:T(8,128)(2,1)}), bf16[1,4,2,32,128]{4,3,2,0,1:T(8,128)(2,1)S(1)}, u32[]{:S(2)}, u32[]{:S(2)}) async-start(bf16[1,4,2,32,128]{4,3,2,0,1:T(8,128)(2,1)} %copy.56), calls=%async_computation.3 | async-start | bytes 131072 | tf_op jit(solution)/shard_map/all_to_all | solution.py:44
  81.9 0.0 collective-permute-done.2
  81.9 0.7 fusion.69
  82.6 3.4 %all-to-all-done.3 = bf16[1,4,2,32,128]{4,3,2,0,1:T(8,128)(2,1)S(1)} async-done(((bf16[1,4,2,32,128]{4,3,2,0,1:T(8,128)(2,1)}), bf16[1,4,2,32,128]{4,3,2,0,1:T(8,128)(2,1)S(1)}, u32[]{:S(2)}, u32[]{:S(2)}) %all-to-all-start.3) | async-done | bytes 65568 | tf_op jit(solution)/shard_map/all_to_all | solution.py:44
  86.0 0.2 convolution_bitcast_fusion.6
  86.2 0.7 fusion.56
  (22 shorter events, 0.3 us)
Async XLA Ops:
  0.6 11.6 %copy-start = (bf16[1,1,4,2,128,256]{5,4,3,2,1,0:T(8,128)(2,1)S(1)}, bf16[1,1,4,2,128,256]{5,4,3,2,1,0:T(8,128)(2,1)}, u32[]{:S(2)}) copy-start(bf16[1,1,4,2,128,256]{5,4,3,2,1,0:T(8,128)(2,1)} %param.9) | copy-start | bytes 1572868
  0.6 0.7 copy-start.3
  1.4 2.1 %copy-start.1 = (bf16[1,2,32,256]{3,2,1,0:T(8,128)(2,1)S(1)}, bf16[1,2,32,256]{3,2,1,0:T(8,128)(2,1)}, u32[]{:S(2)}) copy-start(bf16[1,2,32,256]{3,2,1,0:T(8,128)(2,1)} %param.6) | copy-start | bytes 98308
  2.2 14.8 %collective-permute-start.3 = (bf16[2,32,256]{2,1,0:T(8,128)(2,1)S(1)}, bf16[2,32,256]{2,1,0:T(8,128)(2,1)S(1)}, u32[]{:S(2)}, u32[]{:S(2)}) collective-permute-start(bf16[2,32,256]{2,1,0:T(8,128)(2,1)S(1)} %bitcast_select_fusion), channel_id=1, source_target_pairs={{4,0},{8,4},{12,8},{16,12},{20,16},{24,20},{28,24},{5,1},{9,5},{13... | collective-permute-start | bytes 98312 | tf_op jit(solution)/shard_map/ppermute | solution.py:12
  11.5 0.7 copy-start.4
  12.5 6.4 %collective-permute-start = (f32[2,32,256]{2,1,0:T(8,128)S(1)}, f32[2,32,256]{2,1,0:T(8,128)S(1)}, u32[]{:S(2)}, u32[]{:S(2)}) collective-permute-start(f32[2,32,256]{2,1,0:T(8,128)S(1)} %maximum_bitcast_fusion), channel_id=1, source_target_pairs={{0,4},{4,8},{8,12},{12,16},{16,20},{20,24},{24,28},{1,5},{5,9},{9,... | collective-permute-start | bytes 196616 | tf_op jit(solution)/shard_map/ppermute | solution.py:12
  26.1 8.7 %collective-permute-start.1 = (f32[2,32,256]{2,1,0:T(8,128)S(1)}, f32[2,32,256]{2,1,0:T(8,128)S(1)}, u32[]{:S(2)}, u32[]{:S(2)}) collective-permute-start(f32[2,32,256]{2,1,0:T(8,128)S(1)} %maximum_bitcast_fusion.1), channel_id=1, source_target_pairs={{0,4},{4,8},{8,12},{12,16},{16,20},{20,24},{24,28},{1,5},{5,9},{9,... | collective-permute-start | bytes 196616 | tf_op jit(solution)/shard_map/ppermute | solution.py:12
  31.4 7.4 %all-to-all-start = ((bf16[1,4,2,32,128]{4,3,2,0,1:T(8,128)(2,1)}), bf16[1,4,2,32,128]{4,3,2,0,1:T(8,128)(2,1)S(1)}, u32[]{:S(2)}, u32[]{:S(2)}) async-start(bf16[1,4,2,32,128]{4,3,2,0,1:T(8,128)(2,1)} %copy.49), calls=%async_computation | async-start | bytes 131072 | tf_op jit(solution)/shard_map/all_to_all | solution.py:44
  38.8 15.2 %all-to-all-start.1 = ((bf16[1,4,2,128,256]{4,3,2,0,1:T(8,128)(2,1)}), bf16[1,4,2,128,256]{4,3,2,0,1:T(8,128)(2,1)S(1)}, u32[]{:S(2)}, u32[]{:S(2)}) async-start(bf16[1,4,2,128,256]{4,3,2,0,1:T(8,128)(2,1)} %bitcast.74), calls=%async_computation.1 | async-start | bytes 1048576 | tf_op jit(solution)/shard_map/all_to_all | solution.py:67
  54.3 0.8 copy-start.2
  55.1 7.1 %collective-permute-start.4 = (bf16[2,32,256]{2,1,0:T(8,128)(2,1)S(1)}, bf16[2,32,256]{2,1,0:T(8,128)(2,1)S(1)}, u32[]{:S(2)}, u32[]{:S(2)}) collective-permute-start(bf16[2,32,256]{2,1,0:T(8,128)(2,1)S(1)} %fusion.31), channel_id=1, source_target_pairs={{4,0},{8,4},{12,8},{16,12},{20,16},{24,20},{28,24},{5,1},{9,5},{13... | collective-permute-start | bytes 98312 | tf_op jit(solution)/shard_map/ppermute | solution.py:12
  63.2 7.4 %all-to-all-start.2 = ((bf16[1,4,2,32,128]{4,3,2,0,1:T(8,128)(2,1)}), bf16[1,4,2,32,128]{4,3,2,0,1:T(8,128)(2,1)S(1)}, u32[]{:S(2)}, u32[]{:S(2)}) async-start(bf16[1,4,2,32,128]{4,3,2,0,1:T(8,128)(2,1)} %copy.53), calls=%async_computation.2 | async-start | bytes 131072 | tf_op jit(solution)/shard_map/all_to_all | solution.py:44
  70.9 6.8 %collective-permute-start.5 = (bf16[2,32,256]{2,1,0:T(8,128)(2,1)S(1)}, bf16[2,32,256]{2,1,0:T(8,128)(2,1)S(1)}, u32[]{:S(2)}, u32[]{:S(2)}) collective-permute-start(bf16[2,32,256]{2,1,0:T(8,128)(2,1)S(1)} %fusion.32), channel_id=1, source_target_pairs={{4,0},{8,4},{12,8},{16,12},{20,16},{24,20},{28,24},{5,1},{9,5},{13... | collective-permute-start | bytes 98312 | tf_op jit(solution)/shard_map/ppermute | solution.py:12
  72.2 9.7 %collective-permute-start.2 = (f32[2,32,256]{2,1,0:T(8,128)S(1)}, f32[2,32,256]{2,1,0:T(8,128)S(1)}, u32[]{:S(2)}, u32[]{:S(2)}) collective-permute-start(f32[2,32,256]{2,1,0:T(8,128)S(1)} %maximum_bitcast_fusion.2), channel_id=1, source_target_pairs={{0,4},{4,8},{8,12},{12,16},{16,20},{20,24},{24,28},{1,5},{5,9},{9,... | collective-permute-start | bytes 196616 | tf_op jit(solution)/shard_map/ppermute | solution.py:12
  78.6 7.4 %all-to-all-start.3 = ((bf16[1,4,2,32,128]{4,3,2,0,1:T(8,128)(2,1)}), bf16[1,4,2,32,128]{4,3,2,0,1:T(8,128)(2,1)S(1)}, u32[]{:S(2)}, u32[]{:S(2)}) async-start(bf16[1,4,2,32,128]{4,3,2,0,1:T(8,128)(2,1)} %copy.56), calls=%async_computation.3 | async-start | bytes 131072 | tf_op jit(solution)/shard_map/all_to_all | solution.py:44
where the time goes:
time: 87.8 us; the launch traced here: 86.9 us
  starting transfers between devices  31.9 us (36%)
  blocking collectives  22.2 us (25%)
  waiting for transfers between devices  18.6 us (21%)
  matrix products  6 us (7%)
  local copies, waits for them, and re-layouts  4.16 us (5%)
  other arithmetic  3 us (3%)
  between operations  1.02 us (1%)
    all_gather x3, blocking collectives, advance(): gathered = lax.all_gather(up_part, 'xy', axis=2, tiled=True)  22.2 us
    ppermute x6, starting transfers between devices, from_behind(): return lax.ppermute(block, axis, route)  18.5 us
    all_to_all x3, waiting for transfers between devices, advance(): lax.all_to_all(down_coef, 'xy', split_axis=1, concat_axis=0, tiled=True)  11.4 us
    all_to_all x3, starting transfers between devices, advance(): lax.all_to_all(down_coef, 'xy', split_axis=1, concat_axis=0, tiled=True)  9.85 us
    ppermute x6, waiting for transfers between devices, from_behind(): return lax.ppermute(block, axis, route)  7.18 us
    dot_general x3, matrix products, advance(): jnp.einsum('asjb,ijcrb->ijascr', pieces, v_layer, preferred_element_type=...  3.95 us
    all_to_all x1, starting transfers between devices, on_device(): lax.all_to_all(v_layer, 'xy', split_axis=1, concat_axis=0, tiled=True)  3.47 us
    unnamed x10, local copies, waits for them, and re-layouts  2.08 us
  transfers between devices with their start and end apart: 10, of which 5 were waited for; matrix products, arithmetic and copies ran while one was open for 7% of the time, Pallas kernels for 0%

commit v1 on v0

--- a/solution.py
+++ b/solution.py
@@ -23,7 +23,12 @@
     own_rows = u_layer.shape[0]
     blocks = u_layer.shape[1]
     width = u_layer.shape[-1]
-    gathered = lax.all_gather(up_part, "xy", axis=2, tiled=True)
+    ring = [up_part]
+    for hop in range(3):
+        ring.append(lax.ppermute(ring[-1], "xy", [(dev, (dev + 1) % 4) for dev in range(4)]))
+    gathered = jnp.roll(
+        jnp.concatenate(ring[::-1], axis=2), (lax.axis_index("xy") + 1) * ring[0].shape[2], axis=2
+    )
     pieces = gathered.reshape(2, sources, blocks, width)
     up_coef = complex_parts(
         jnp.einsum("asjb,ijcrb->ijascr", pieces, v_layer, preferred_element_type=jnp.float32)

time: 87.8 us -> 81.5 us (0.928)
  blocking collectives: 22.2 us -> 0 us
  waiting for transfers between devices: 18.6 us -> 34.1 us
  local copies, waits for them, and re-layouts: 4.16 us -> 2.85 us
  starting transfers between devices: 31.9 us -> 33 us
    all_gather x3 -> x0, blocking collectives: 22.2 us -> none  [advance(): gathered = lax.all_gather(up_part, 'xy', axis=2, tiled=True)]
    ppermute x0 -> x9, waiting for transfers between devices: none -> 19.8 us  [advance(): lax.ppermute(ring[-1], 'xy', [(dev, (dev + 1) % 4) for dev in range(4)])]
    all_to_all x3, waiting for transfers between devices: 11.4 us -> 7.73 us  [advance(): lax.all_to_all(down_coef, 'xy', split_axis=1, concat_axis=0, tiled=True)]
    ppermute x0 -> x9, starting transfers between devices: none -> 1.46 us  [advance(): lax.ppermute(ring[-1], 'xy', [(dev, (dev + 1) % 4) for dev in range(4)])]
    unnamed x10, local copies, waits for them, and re-layouts: 2.08 us -> 0.73 us
  transfers between devices with their start and end apart: 10 -> 19, of which waited for: 5 -> 13; matrix products, arithmetic and copies ran while one was open for 7% -> 12% of each run, Pallas kernels for 0% -> 0%
where the time goes in v1:
time: 81.5 us; the launch traced here: 80.7 us
  waiting for transfers between devices  34.1 us (42%)
  starting transfers between devices  33 us (40%)
  matrix products  6 us (7%)
  other arithmetic  3.67 us (5%)
  local copies, waits for them, and re-layouts  2.85 us (3%)
  between operations  1.04 us (1%)
    ppermute x9, waiting for transfers between devices, advance(): lax.ppermute(ring[-1], 'xy', [(dev, (dev + 1) % 4) for dev in range(4)])  19.8 us
    ppermute x6, starting transfers between devices, from_behind(): return lax.ppermute(block, axis, route)  18.3 us
    all_to_all x3, starting transfers between devices, advance(): lax.all_to_all(down_coef, 'xy', split_axis=1, concat_axis=0, tiled=True)  9.85 us
    all_to_all x3, waiting for transfers between devices, advance(): lax.all_to_all(down_coef, 'xy', split_axis=1, concat_axis=0, tiled=True)  7.73 us
    ppermute x6, waiting for transfers between devices, from_behind(): return lax.ppermute(block, axis, route)  6.52 us
    dot_general x3, matrix products, advance(): jnp.einsum('asjb,ijcrb->ijascr', pieces, v_layer, preferred_element_type=...  3.96 us
    all_to_all x1, starting transfers between devices, on_device(): lax.all_to_all(v_layer, 'xy', split_axis=1, concat_axis=0, tiled=True)  3.47 us
    convert_element_type x3, local copies, waits for them, and re-layouts, advance(): jnp.where(keep_rank[:, :, None, None, :], down_coef, 0.0)  1.89 us
  transfers between devices with their start and end apart: 19, of which 13 were waited for; matrix products, arithmetic and copies ran while one was open for 12% of the time, Pallas kernels for 0%

profile of v1, /device:TPU:0, one launch (start us, length us, event | category | flops | bytes accessed | tf_op | source)
XLA Modules:
  0.0 80.7 jit_solution(4133404045909280844)
XLA Ops:
  0.6 0.0 copy-start
  0.7 0.7 copy-done.3
  1.4 0.8 %bitcast_select_fusion.1 = bf16[2,32,256]{2,1,0:T(8,128)(2,1)S(1)} fusion(bf16[1,2,32,256]{3,2,1,0:T(8,128)(2,1)} %param.8, pred[32]{0:T(512)(128)(4,1)S(1)} %get-tuple-element.24), kind=kLoop, calls=%fused_computation.183 | loop fusion | flops 16384 | bytes 65568 | tf_op jit(solution)/shard_map/jit(_where)/select_n | solution.py:62
  2.2 0.5 collective-permute-start
  2.7 0.1 bitcast_select_fusion
  2.8 1.3 %collective-permute-start.12 = (bf16[2,32,256]{2,1,0:T(8,128)(2,1)S(1)}, bf16[2,32,256]{2,1,0:T(8,128)(2,1)S(1)}, u32[]{:S(2)}, u32[]{:S(2)}) collective-permute-start(bf16[2,32,256]{2,1,0:T(8,128)(2,1)S(1)} %bitcast_select_fusion), channel_id=1, source_target_pairs={{4,0},{8,4},{12,8},{16,12},{20,16},{24,20},{28,24},{5,1},{9,5},{13... | collective-permute-start | bytes 98312 | tf_op jit(solution)/shard_map/ppermute | solution.py:12
  4.1 2.1 %collective-permute-done = bf16[2,32,256]{2,1,0:T(8,128)(2,1)S(1)} collective-permute-done((bf16[2,32,256]{2,1,0:T(8,128)(2,1)S(1)}, bf16[2,32,256]{2,1,0:T(8,128)(2,1)S(1)}, u32[]{:S(2)}, u32[]{:S(2)}) %collective-permute-start) | collective-permute-done | bytes 32800 | tf_op jit(solution)/shard_map/ppermute | solution.py:28
  6.2 0.5 collective-permute-start.1
  6.7 2.8 %collective-permute-done.1 = bf16[2,32,256]{2,1,0:T(8,128)(2,1)S(1)} collective-permute-done((bf16[2,32,256]{2,1,0:T(8,128)(2,1)S(1)}, bf16[2,32,256]{2,1,0:T(8,128)(2,1)S(1)}, u32[]{:S(2)}, u32[]{:S(2)}) %collective-permute-start.1) | collective-permute-done | bytes 32800 | tf_op jit(solution)/shard_map/ppermute | solution.py:28
  9.6 0.1 collective-permute-start.2
  9.7 0.1 iota_compare_fusion
  9.7 3.2 %collective-permute-done.2 = bf16[2,32,256]{2,1,0:T(8,128)(2,1)S(1)} collective-permute-done((bf16[2,32,256]{2,1,0:T(8,128)(2,1)S(1)}, bf16[2,32,256]{2,1,0:T(8,128)(2,1)S(1)}, u32[]{:S(2)}, u32[]{:S(2)}) %collective-permute-start.2) | collective-permute-done | bytes 32800 | tf_op jit(solution)/shard_map/ppermute | solution.py:28
  12.9 0.2 fusion.39
  13.1 0.1 reshape.884
  13.2 1.3 %convolution_bitcast_fusion.5 = f32[1,4,2,32,2,128]{5,3,4,2,1,0:T(8,128)S(1)} fusion(bf16[1,1,4,2,128,256]{5,4,3,2,1,0:T(8,128)(2,1)} %param.12, bf16[2,32,4,256,1]{3,2,1,0,4:T(4,128)(2,1)S(1)} %bitcast.274), kind=kOutput, calls=%fused_computation.5 | convolution fusion | flops 33554432 | bytes 917504 | tf_op jit(solution)/shard_map/asjb,ijcrb->ijascr/dot_general | solution.py:34
  14.6 0.2 convolution_bitcast_fusion.11
  14.8 0.0 copy-start.1
  14.8 4.2 %collective-permute-start.3 = (f32[2,32,256]{2,1,0:T(8,128)S(1)}, f32[2,32,256]{2,1,0:T(8,128)S(1)}, u32[]{:S(2)}, u32[]{:S(2)}) collective-permute-start(f32[2,32,256]{2,1,0:T(8,128)S(1)} %maximum_bitcast_fusion), channel_id=1, source_target_pairs={{0,4},{4,8},{8,12},{12,16},{16,20},{20,24},{24,28},{1,5},{5,9},{9,... | collective-permute-start | bytes 196616 | tf_op jit(solution)/shard_map/ppermute | solution.py:12
  19.1 0.3 convolution_bitcast_fusion.2
  19.4 1.6 %collective-permute-done.3 = f32[2,32,256]{2,1,0:T(8,128)S(1)} collective-permute-done((f32[2,32,256]{2,1,0:T(8,128)S(1)}, f32[2,32,256]{2,1,0:T(8,128)S(1)}, u32[]{:S(2)}, u32[]{:S(2)}) %collective-permute-start.3) | collective-permute-done | bytes 65568 | tf_op jit(solution)/shard_map/ppermute | solution.py:12
  21.0 0.1 fusion.54
  21.0 0.0 collective-permute-start.4
  21.1 3.3 %collective-permute-done.4 = bf16[2,32,256]{2,1,0:T(8,128)(2,1)S(1)} collective-permute-done((bf16[2,32,256]{2,1,0:T(8,128)(2,1)S(1)}, bf16[2,32,256]{2,1,0:T(8,128)(2,1)S(1)}, u32[]{:S(2)}, u32[]{:S(2)}) %collective-permute-start.4) | collective-permute-done | bytes 32800 | tf_op jit(solution)/shard_map/ppermute | solution.py:28
  24.4 3.3 %collective-permute-done.5 = bf16[2,32,256]{2,1,0:T(8,128)(2,1)S(1)} collective-permute-done((bf16[2,32,256]{2,1,0:T(8,128)(2,1)S(1)}, bf16[2,32,256]{2,1,0:T(8,128)(2,1)S(1)}, u32[]{:S(2)}, u32[]{:S(2)}) %collective-permute-start.5) | collective-permute-done | bytes 32800 | tf_op jit(solution)/shard_map/ppermute | solution.py:28
  27.7 0.6 copy.47
  28.4 3.3 %all-to-all-start = ((bf16[1,4,2,32,128]{4,3,2,0,1:T(8,128)(2,1)}), bf16[1,4,2,32,128]{4,3,2,0,1:T(8,128)(2,1)S(1)}, u32[]{:S(2)}, u32[]{:S(2)}) async-start(bf16[1,4,2,32,128]{4,3,2,0,1:T(8,128)(2,1)} %copy.47), calls=%async_computation | async-start | bytes 131072 | tf_op jit(solution)/shard_map/all_to_all | solution.py:49
  31.7 0.0 collective-permute-done.6
  31.7 0.2 fusion.32
  31.9 0.1 reshape.887
  32.0 1.3 %convolution_bitcast_fusion.4 = f32[1,4,2,32,2,128]{5,3,1,4,2,0:T(8,128)S(1)} fusion(bf16[2,32,4,256,1]{3,2,1,0,4:T(4,128)(2,1)S(1)} %bitcast.275, bf16[1,1,4,2,128,256]{5,4,3,2,1,0:T(8,128)(2,1)} %param.12), kind=kOutput, calls=%fused_computation.4 | convolution fusion | flops 33554432 | bytes 917504 | tf_op jit(solution)/shard_map/asjb,ijcrb->ijascr/dot_general | solution.py:34
  33.4 0.2 convolution_bitcast_fusion.10
  33.6 2.2 %all-to-all-done = bf16[1,4,2,32,128]{4,3,2,0,1:T(8,128)(2,1)S(1)} async-done(((bf16[1,4,2,32,128]{4,3,2,0,1:T(8,128)(2,1)}), bf16[1,4,2,32,128]{4,3,2,0,1:T(8,128)(2,1)S(1)}, u32[]{:S(2)}, u32[]{:S(2)}) %all-to-all-start) | async-done | bytes 65568 | tf_op jit(solution)/shard_map/all_to_all | solution.py:49
  35.8 3.5 %all-to-all-start.1 = ((bf16[1,4,2,128,256]{4,3,2,0,1:T(8,128)(2,1)}), bf16[1,4,2,128,256]{4,3,2,0,1:T(8,128)(2,1)S(1)}, u32[]{:S(2)}, u32[]{:S(2)}) async-start(bf16[1,4,2,128,256]{4,3,2,0,1:T(8,128)(2,1)} %bitcast.74), calls=%async_computation.1 | async-start | bytes 1048576 | tf_op jit(solution)/shard_map/all_to_all | solution.py:72
  39.2 4.3 %collective-permute-start.7 = (f32[2,32,256]{2,1,0:T(8,128)S(1)}, f32[2,32,256]{2,1,0:T(8,128)S(1)}, u32[]{:S(2)}, u32[]{:S(2)}) collective-permute-start(f32[2,32,256]{2,1,0:T(8,128)S(1)} %maximum_bitcast_fusion.1), channel_id=1, source_target_pairs={{0,4},{4,8},{8,12},{12,16},{16,20},{20,24},{24,28},{1,5},{5,9},{9,... | collective-permute-start | bytes 196616 | tf_op jit(solution)/shard_map/ppermute | solution.py:12
  43.5 1.9 %collective-permute-done.7 = f32[2,32,256]{2,1,0:T(8,128)S(1)} collective-permute-done((f32[2,32,256]{2,1,0:T(8,128)S(1)}, f32[2,32,256]{2,1,0:T(8,128)S(1)}, u32[]{:S(2)}, u32[]{:S(2)}) %collective-permute-start.7) | collective-permute-done | bytes 65568 | tf_op jit(solution)/shard_map/ppermute | solution.py:12
  45.5 0.1 fusion.55
  45.6 3.3 %collective-permute-done.8 = bf16[2,32,256]{2,1,0:T(8,128)(2,1)S(1)} collective-permute-done((bf16[2,32,256]{2,1,0:T(8,128)(2,1)S(1)}, bf16[2,32,256]{2,1,0:T(8,128)(2,1)S(1)}, u32[]{:S(2)}, u32[]{:S(2)}) %collective-permute-start.8) | collective-permute-done | bytes 32800 | tf_op jit(solution)/shard_map/ppermute | solution.py:28
  48.9 0.0 collective-permute-start.9
  48.9 0.2 convolution_bitcast_fusion.8
  49.1 0.1 fusion.52
  49.2 1.3 %collective-permute-start.13 = (bf16[2,32,256]{2,1,0:T(8,128)(2,1)S(1)}, bf16[2,32,256]{2,1,0:T(8,128)(2,1)S(1)}, u32[]{:S(2)}, u32[]{:S(2)}) collective-permute-start(bf16[2,32,256]{2,1,0:T(8,128)(2,1)S(1)} %fusion.52), channel_id=1, source_target_pairs={{4,0},{8,4},{12,8},{16,12},{20,16},{24,20},{28,24},{5,1},{9,5},{13... | collective-permute-start | bytes 98312 | tf_op jit(solution)/shard_map/ppermute | solution.py:12
  50.5 1.7 %collective-permute-done.9 = bf16[2,32,256]{2,1,0:T(8,128)(2,1)S(1)} collective-permute-done((bf16[2,32,256]{2,1,0:T(8,128)(2,1)S(1)}, bf16[2,32,256]{2,1,0:T(8,128)(2,1)S(1)}, u32[]{:S(2)}, u32[]{:S(2)}) %collective-permute-start.9) | collective-permute-done | bytes 32800 | tf_op jit(solution)/shard_map/ppermute | solution.py:28
  52.2 0.3 collective-permute-start.10
  52.6 3.0 %collective-permute-done.13 = bf16[2,32,256]{2,1,0:T(8,128)(2,1)S(1)} collective-permute-done((bf16[2,32,256]{2,1,0:T(8,128)(2,1)S(1)}, bf16[2,32,256]{2,1,0:T(8,128)(2,1)S(1)}, u32[]{:S(2)}, u32[]{:S(2)}) %collective-permute-start.13) | collective-permute-done | bytes 32800 | tf_op jit(solution)/shard_map/ppermute | solution.py:12
  55.5 0.3 convolution_bitcast_fusion.1
  55.9 0.6 copy.51
  56.5 3.3 %all-to-all-start.2 = ((bf16[1,4,2,32,128]{4,3,2,0,1:T(8,128)(2,1)}), bf16[1,4,2,32,128]{4,3,2,0,1:T(8,128)(2,1)S(1)}, u32[]{:S(2)}, u32[]{:S(2)}) async-start(bf16[1,4,2,32,128]{4,3,2,0,1:T(8,128)(2,1)} %copy.51), calls=%async_computation.2 | async-start | bytes 131072 | tf_op jit(solution)/shard_map/all_to_all | solution.py:49
  59.8 0.2 fusion.25
  60.0 0.1 reshape.888
  60.1 1.3 %convolution_bitcast_fusion.3 = f32[1,4,2,32,2,128]{5,3,1,4,2,0:T(8,128)S(1)} fusion(bf16[2,32,4,256,1]{3,2,1,0,4:T(4,128)(2,1)S(1)} %bitcast.276, bf16[1,1,4,2,128,256]{5,4,3,2,1,0:T(8,128)(2,1)} %param.12), kind=kOutput, calls=%fused_computation.3 | convolution fusion | flops 33554432 | bytes 917504 | tf_op jit(solution)/shard_map/asjb,ijcrb->ijascr/dot_general | solution.py:34
  61.5 0.2 convolution_bitcast_fusion.9
  61.7 2.2 %all-to-all-done.2 = bf16[1,4,2,32,128]{4,3,2,0,1:T(8,128)(2,1)S(1)} async-done(((bf16[1,4,2,32,128]{4,3,2,0,1:T(8,128)(2,1)}), bf16[1,4,2,32,128]{4,3,2,0,1:T(8,128)(2,1)S(1)}, u32[]{:S(2)}, u32[]{:S(2)}) %all-to-all-start.2) | async-done | bytes 65568 | tf_op jit(solution)/shard_map/all_to_all | solution.py:49
  63.9 0.2 convolution_bitcast_fusion.7
  64.1 0.1 fusion.53
  64.2 1.3 %collective-permute-start.14 = (bf16[2,32,256]{2,1,0:T(8,128)(2,1)S(1)}, bf16[2,32,256]{2,1,0:T(8,128)(2,1)S(1)}, u32[]{:S(2)}, u32[]{:S(2)}) collective-permute-start(bf16[2,32,256]{2,1,0:T(8,128)(2,1)S(1)} %fusion.53), channel_id=1, source_target_pairs={{4,0},{8,4},{12,8},{16,12},{20,16},{24,20},{28,24},{5,1},{9,5},{13... | collective-permute-start | bytes 98312 | tf_op jit(solution)/shard_map/ppermute | solution.py:12
  65.5 5.9 %collective-permute-start.11 = (f32[2,32,256]{2,1,0:T(8,128)S(1)}, f32[2,32,256]{2,1,0:T(8,128)S(1)}, u32[]{:S(2)}, u32[]{:S(2)}) collective-permute-start(f32[2,32,256]{2,1,0:T(8,128)S(1)} %maximum_bitcast_fusion.2), channel_id=1, source_target_pairs={{0,4},{4,8},{8,12},{12,16},{16,20},{20,24},{24,28},{1,5},{5,9},{9,... | collective-permute-start | bytes 196616 | tf_op jit(solution)/shard_map/ppermute | solution.py:12
  71.4 0.0 collective-permute-done.14
  71.4 0.3 convolution_bitcast_fusion
  71.8 0.6 copy.54
  72.4 3.3 %all-to-all-start.3 = ((bf16[1,4,2,32,128]{4,3,2,0,1:T(8,128)(2,1)}), bf16[1,4,2,32,128]{4,3,2,0,1:T(8,128)(2,1)S(1)}, u32[]{:S(2)}, u32[]{:S(2)}) async-start(bf16[1,4,2,32,128]{4,3,2,0,1:T(8,128)(2,1)} %copy.54), calls=%async_computation.3 | async-start | bytes 131072 | tf_op jit(solution)/shard_map/all_to_all | solution.py:49
  75.7 0.7 fusion.90
  76.4 3.4 %all-to-all-done.3 = bf16[1,4,2,32,128]{4,3,2,0,1:T(8,128)(2,1)S(1)} async-done(((bf16[1,4,2,32,128]{4,3,2,0,1:T(8,128)(2,1)}), bf16[1,4,2,32,128]{4,3,2,0,1:T(8,128)(2,1)S(1)}, u32[]{:S(2)}, u32[]{:S(2)}) %all-to-all-start.3) | async-done | bytes 65568 | tf_op jit(solution)/shard_map/all_to_all | solution.py:49
  79.8 0.2 convolution_bitcast_fusion.6
  80.0 0.7 fusion.77
  (36 shorter events, 0.3 us)
Async XLA Ops:
  0.6 13.9 %copy-start = (bf16[1,1,4,2,128,256]{5,4,3,2,1,0:T(8,128)(2,1)S(1)}, bf16[1,1,4,2,128,256]{5,4,3,2,1,0:T(8,128)(2,1)}, u32[]{:S(2)}) copy-start(bf16[1,1,4,2,128,256]{5,4,3,2,1,0:T(8,128)(2,1)} %param.11) | copy-start | bytes 1572868
  0.7 0.7 copy-start.3
  1.4 1.3 %copy-start.2 = (bf16[1,2,32,256]{3,2,1,0:T(8,128)(2,1)S(1)}, bf16[1,2,32,256]{3,2,1,0:T(8,128)(2,1)}, u32[]{:S(2)}) copy-start(bf16[1,2,32,256]{3,2,1,0:T(8,128)(2,1)} %param.9) | copy-start | bytes 98308
  2.2 4.0 %collective-permute-start = (bf16[2,32,256]{2,1,0:T(8,128)(2,1)S(1)}, bf16[2,32,256]{2,1,0:T(8,128)(2,1)S(1)}, u32[]{:S(2)}, u32[]{:S(2)}) collective-permute-start(bf16[2,32,256]{2,1,0:T(8,128)(2,1)S(1)} %bitcast_select_fusion.1), channel_id=1, source_target_pairs={{0,1},{1,2},{2,3},{3,0},{4,5},{5,6},{6,7},{7,4},{8,9},{9,10},{10,1... | collective-permute-start | bytes 98312 | tf_op jit(solution)/shard_map/ppermute | solution.py:28
  2.7 4.0 %copy-start.4 = (s32[1,1,4]{2,1,0:T(1,128)S(1)}, s32[1,1,4]{2,1,0:T(1,128)}, u32[]{:S(2)}) copy-start(s32[1,1,4]{2,1,0:T(1,128)} %param.13) | copy-start | bytes 52
  2.8 16.3 %collective-permute-start.12 = (bf16[2,32,256]{2,1,0:T(8,128)(2,1)S(1)}, bf16[2,32,256]{2,1,0:T(8,128)(2,1)S(1)}, u32[]{:S(2)}, u32[]{:S(2)}) collective-permute-start(bf16[2,32,256]{2,1,0:T(8,128)(2,1)S(1)} %bitcast_select_fusion), channel_id=1, source_target_pairs={{4,0},{8,4},{12,8},{16,12},{20,16},{24,20},{28,24},{5,1},{9,5},{13... | collective-permute-start | bytes 98312 | tf_op jit(solution)/shard_map/ppermute | solution.py:12
  6.2 3.3 %collective-permute-start.1 = (bf16[2,32,256]{2,1,0:T(8,128)(2,1)S(1)}, bf16[2,32,256]{2,1,0:T(8,128)(2,1)S(1)}, u32[]{:S(2)}, u32[]{:S(2)}) collective-permute-start(bf16[2,32,256]{2,1,0:T(8,128)(2,1)S(1)} %collective-permute-done), channel_id=1, source_target_pairs={{0,1},{1,2},{2,3},{3,0},{4,5},{5,6},{6,7},{7,4},{8,9},{9,10},{10,1... | collective-permute-start | bytes 98312 | tf_op jit(solution)/shard_map/ppermute | solution.py:28
  9.6 3.3 %collective-permute-start.2 = (bf16[2,32,256]{2,1,0:T(8,128)(2,1)S(1)}, bf16[2,32,256]{2,1,0:T(8,128)(2,1)S(1)}, u32[]{:S(2)}, u32[]{:S(2)}) collective-permute-start(bf16[2,32,256]{2,1,0:T(8,128)(2,1)S(1)} %collective-permute-done.1), channel_id=1, source_target_pairs={{0,1},{1,2},{2,3},{3,0},{4,5},{5,6},{6,7},{7,4},{8,9},{9,10},{10,1... | collective-permute-start | bytes 98312 | tf_op jit(solution)/shard_map/ppermute | solution.py:28
  14.8 6.1 %copy-start.1 = (bf16[1,2,32,256]{3,2,1,0:T(8,128)(2,1)S(1)}, bf16[1,2,32,256]{3,2,1,0:T(8,128)(2,1)}, u32[]{:S(2)}) copy-start(bf16[1,2,32,256]{3,2,1,0:T(8,128)(2,1)} %param.8) | copy-start | bytes 98308
  14.8 6.1 %collective-permute-start.3 = (f32[2,32,256]{2,1,0:T(8,128)S(1)}, f32[2,32,256]{2,1,0:T(8,128)S(1)}, u32[]{:S(2)}, u32[]{:S(2)}) collective-permute-start(f32[2,32,256]{2,1,0:T(8,128)S(1)} %maximum_bitcast_fusion), channel_id=1, source_target_pairs={{0,4},{4,8},{8,12},{12,16},{16,20},{20,24},{24,28},{1,5},{5,9},{9,... | collective-permute-start | bytes 196616 | tf_op jit(solution)/shard_map/ppermute | solution.py:12
  21.0 3.3 %collective-permute-start.4 = (bf16[2,32,256]{2,1,0:T(8,128)(2,1)S(1)}, bf16[2,32,256]{2,1,0:T(8,128)(2,1)S(1)}, u32[]{:S(2)}, u32[]{:S(2)}) collective-permute-start(bf16[2,32,256]{2,1,0:T(8,128)(2,1)S(1)} %fusion.54), channel_id=1, source_target_pairs={{0,1},{1,2},{2,3},{3,0},{4,5},{5,6},{6,7},{7,4},{8,9},{9,10},{10,1... | collective-permute-start | bytes 98312 | tf_op jit(solution)/shard_map/ppermute | solution.py:28
  24.4 3.3 %collective-permute-start.5 = (bf16[2,32,256]{2,1,0:T(8,128)(2,1)S(1)}, bf16[2,32,256]{2,1,0:T(8,128)(2,1)S(1)}, u32[]{:S(2)}, u32[]{:S(2)}) collective-permute-start(bf16[2,32,256]{2,1,0:T(8,128)(2,1)S(1)} %collective-permute-done.4), channel_id=1, source_target_pairs={{0,1},{1,2},{2,3},{3,0},{4,5},{5,6},{6,7},{7,4},{8,9},{9,10},{10,1... | collective-permute-start | bytes 98312 | tf_op jit(solution)/shard_map/ppermute | solution.py:28
  27.7 3.9 %collective-permute-start.6 = (bf16[2,32,256]{2,1,0:T(8,128)(2,1)S(1)}, bf16[2,32,256]{2,1,0:T(8,128)(2,1)S(1)}, u32[]{:S(2)}, u32[]{:S(2)}) collective-permute-start(bf16[2,32,256]{2,1,0:T(8,128)(2,1)S(1)} %collective-permute-done.5), channel_id=1, source_target_pairs={{0,1},{1,2},{2,3},{3,0},{4,5},{5,6},{6,7},{7,4},{8,9},{9,10},{10,1... | collective-permute-start | bytes 98312 | tf_op jit(solution)/shard_map/ppermute | solution.py:28
  28.4 7.4 %all-to-all-start = ((bf16[1,4,2,32,128]{4,3,2,0,1:T(8,128)(2,1)}), bf16[1,4,2,32,128]{4,3,2,0,1:T(8,128)(2,1)S(1)}, u32[]{:S(2)}, u32[]{:S(2)}) async-start(bf16[1,4,2,32,128]{4,3,2,0,1:T(8,128)(2,1)} %copy.47), calls=%async_computation | async-start | bytes 131072 | tf_op jit(solution)/shard_map/all_to_all | solution.py:49
  35.8 13.1 %all-to-all-start.1 = ((bf16[1,4,2,128,256]{4,3,2,0,1:T(8,128)(2,1)}), bf16[1,4,2,128,256]{4,3,2,0,1:T(8,128)(2,1)S(1)}, u32[]{:S(2)}, u32[]{:S(2)}) async-start(bf16[1,4,2,128,256]{4,3,2,0,1:T(8,128)(2,1)} %bitcast.74), calls=%async_computation.1 | async-start | bytes 1048576 | tf_op jit(solution)/shard_map/all_to_all | solution.py:72
  39.2 6.2 %collective-permute-start.7 = (f32[2,32,256]{2,1,0:T(8,128)S(1)}, f32[2,32,256]{2,1,0:T(8,128)S(1)}, u32[]{:S(2)}, u32[]{:S(2)}) collective-permute-start(f32[2,32,256]{2,1,0:T(8,128)S(1)} %maximum_bitcast_fusion.1), channel_id=1, source_target_pairs={{0,4},{4,8},{8,12},{12,16},{16,20},{20,24},{24,28},{1,5},{5,9},{9,... | collective-permute-start | bytes 196616 | tf_op jit(solution)/shard_map/ppermute | solution.py:12
  45.5 3.3 %collective-permute-start.8 = (bf16[2,32,256]{2,1,0:T(8,128)(2,1)S(1)}, bf16[2,32,256]{2,1,0:T(8,128)(2,1)S(1)}, u32[]{:S(2)}, u32[]{:S(2)}) collective-permute-start(bf16[2,32,256]{2,1,0:T(8,128)(2,1)S(1)} %fusion.55), channel_id=1, source_target_pairs={{0,1},{1,2},{2,3},{3,0},{4,5},{5,6},{6,7},{7,4},{8,9},{9,10},{10,1... | collective-permute-start | bytes 98312 | tf_op jit(solution)/shard_map/ppermute | solution.py:28
  48.9 3.3 %collective-permute-start.9 = (bf16[2,32,256]{2,1,0:T(8,128)(2,1)S(1)}, bf16[2,32,256]{2,1,0:T(8,128)(2,1)S(1)}, u32[]{:S(2)}, u32[]{:S(2)}) collective-permute-start(bf16[2,32,256]{2,1,0:T(8,128)(2,1)S(1)} %collective-permute-done.8), channel_id=1, source_target_pairs={{0,1},{1,2},{2,3},{3,0},{4,5},{5,6},{6,7},{7,4},{8,9},{9,10},{10,1... | collective-permute-start | bytes 98312 | tf_op jit(solution)/shard_map/ppermute | solution.py:28
  49.2 6.3 %collective-permute-start.13 = (bf16[2,32,256]{2,1,0:T(8,128)(2,1)S(1)}, bf16[2,32,256]{2,1,0:T(8,128)(2,1)S(1)}, u32[]{:S(2)}, u32[]{:S(2)}) collective-permute-start(bf16[2,32,256]{2,1,0:T(8,128)(2,1)S(1)} %fusion.52), channel_id=1, source_target_pairs={{4,0},{8,4},{12,8},{16,12},{20,16},{24,20},{28,24},{5,1},{9,5},{13... | collective-permute-start | bytes 98312 | tf_op jit(solution)/shard_map/ppermute | solution.py:12
  52.2 7.6 %collective-permute-start.10 = (bf16[2,32,256]{2,1,0:T(8,128)(2,1)S(1)}, bf16[2,32,256]{2,1,0:T(8,128)(2,1)S(1)}, u32[]{:S(2)}, u32[]{:S(2)}) collective-permute-start(bf16[2,32,256]{2,1,0:T(8,128)(2,1)S(1)} %collective-permute-done.9), channel_id=1, source_target_pairs={{0,1},{1,2},{2,3},{3,0},{4,5},{5,6},{6,7},{7,4},{8,9},{9,10},{10,1... | collective-permute-start | bytes 98312 | tf_op jit(solution)/shard_map/ppermute | solution.py:28
  56.5 7.4 %all-to-all-start.2 = ((bf16[1,4,2,32,128]{4,3,2,0,1:T(8,128)(2,1)}), bf16[1,4,2,32,128]{4,3,2,0,1:T(8,128)(2,1)S(1)}, u32[]{:S(2)}, u32[]{:S(2)}) async-start(bf16[1,4,2,32,128]{4,3,2,0,1:T(8,128)(2,1)} %copy.51), calls=%async_computation.2 | async-start | bytes 131072 | tf_op jit(solution)/shard_map/all_to_all | solution.py:49
  64.2 7.2 %collective-permute-start.14 = (bf16[2,32,256]{2,1,0:T(8,128)(2,1)S(1)}, bf16[2,32,256]{2,1,0:T(8,128)(2,1)S(1)}, u32[]{:S(2)}, u32[]{:S(2)}) collective-permute-start(bf16[2,32,256]{2,1,0:T(8,128)(2,1)S(1)} %fusion.53), channel_id=1, source_target_pairs={{4,0},{8,4},{12,8},{16,12},{20,16},{24,20},{28,24},{5,1},{9,5},{13... | collective-permute-start | bytes 98312 | tf_op jit(solution)/shard_map/ppermute | solution.py:12
  65.5 10.2 %collective-permute-start.11 = (f32[2,32,256]{2,1,0:T(8,128)S(1)}, f32[2,32,256]{2,1,0:T(8,128)S(1)}, u32[]{:S(2)}, u32[]{:S(2)}) collective-permute-start(f32[2,32,256]{2,1,0:T(8,128)S(1)} %maximum_bitcast_fusion.2), channel_id=1, source_target_pairs={{0,4},{4,8},{8,12},{12,16},{16,20},{20,24},{24,28},{1,5},{5,9},{9,... | collective-permute-start | bytes 196616 | tf_op jit(solution)/shard_map/ppermute | solution.py:12
  72.4 7.4 %all-to-all-start.3 = ((bf16[1,4,2,32,128]{4,3,2,0,1:T(8,128)(2,1)}), bf16[1,4,2,32,128]{4,3,2,0,1:T(8,128)(2,1)S(1)}, u32[]{:S(2)}, u32[]{:S(2)}) async-start(bf16[1,4,2,32,128]{4,3,2,0,1:T(8,128)(2,1)} %copy.54), calls=%async_computation.3 | async-start | bytes 131072 | tf_op jit(solution)/shard_map/all_to_all | solution.py:49
